TPU v7x, 512 devices: a whole 4x4x16 slice. The times are simulated.
512 devices in a mesh: tile: 32 (over z, core), chan: 16 (over y, x).
Axes of the slice: x: 4, y: 4, z: 16, core: 2. Of those that a mesh axis runs over, the one named last changes fastest.
Arguments:
- fields: float32 [64, 1024, 411], P('chan', 'tile'), may hold values from -12 to 12
- diffusivity: float32 [64, 1024], P('chan', 'tile'), may hold values from 0.02 to 0.24
- owners: int32 [4096, 1], replicated, may hold values from 0 to 31; in each aligned block of 128 rows (0 to 127, 128 to 255, ...) at most 8 rows name the same one
- observed: bfloat16 [8192, 6144], P('tile', 'chan'), may hold values from -6 to 6
- usable: int32 [8192], P('tile'), may hold values 0 or 1
- w_hidden: bfloat16 [411, 2048], P(None, 'chan'), may hold values from -0.3125 to 0.3125
- b_hidden: float32 [2048], P('chan'), may hold values from -3 to 3
- w_radiance: bfloat16 [2048, 6144], P(None, 'chan'), may hold values from -0.125 to 0.125
- b_radiance: float32 [6144], P('chan'), may hold values from -3 to 3
- inv_cov: bfloat16 [6144, 6144], P('tile', 'chan'), may hold values from -6 to 22
Outputs:
- gradient: float32 [64, 1024, 411], P('chan', 'tile')
Inputs may be any that keep to these rules, and one draw needn't show every extreme that they name: `owners`: in each tile's block of 128 consecutive entries no owner appears more than 8 times, and in some blocks one appears exactly 8 times.
All inputs are finite; a program needn't handle non-finite values. No bound on the sum of `usable` on one device may be relied on, other than what follows from the above.
Results may differ from a plain program's by a relative error of at most 0.0045.
Values may be sent and summed in bfloat16 or wider, within the bound.
A program may use at most 64 MiB of HBM per device.

v0:
```python
import jax
import jax.numpy as jnp
from jax import lax
from jax.sharding import PartitionSpec as P


def padded_2(value, sides, width, wrap):
    for axis, dim in sides:
        devices, length = (lax.axis_size(axis), value.shape[dim])
        up = [(i, (i + 1) % devices) for i in range(devices if wrap else devices - 1)]
        down = [(j, i) for i, j in up]
        last = lax.slice_in_dim(value, length - width, length, axis=dim)
        first = lax.slice_in_dim(value, 0, width, axis=dim)
        before = lax.ppermute(last, axis, up)
        after = lax.ppermute(first, axis, down)
        value = jnp.concatenate([before, value, after], axis=dim)
    return value


def add_rims(values):
    rowwise = padded_2(values, (("chan", 0),), 1, False)
    return padded_2(rowwise, (("tile", 1),), 1, True)


def body(
    fields,
    diffusivity,
    owners,
    observed,
    usable,
    w_hidden,
    b_hidden,
    w_radiance,
    b_radiance,
    inv_cov,
):
    tile_count = lax.axis_size("tile")
    chan_count = lax.axis_size("chan")
    tile_index = lax.axis_index("tile")
    chan_index = lax.axis_index("chan")
    slot_count = observed.shape[0]
    capacity = slot_count // tile_count
    cells_across, cells_along, features = fields.shape
    own_cols = cells_across // 4 * (cells_along // 4)
    tile_cols = chan_count * own_cols
    hidden_dev = w_hidden.shape[1]
    owner_table = owners[:, 0].reshape(tile_count, tile_cols)
    owner_hits = (
        owner_table[:, :, None] == jnp.arange(tile_count, dtype=jnp.int32)[None, None, :]
    ).astype(jnp.int32)
    before = jnp.sum((jnp.cumsum(owner_hits, axis=1) - owner_hits) * owner_hits, axis=2)
    tallies = jnp.sum(owner_hits, axis=1)
    slot_of = lax.dynamic_index_in_dim(
        owner_table * capacity + before, tile_index, 0, keepdims=False
    )
    arriving = lax.dynamic_index_in_dim(tallies, tile_index, 1, keepdims=False)
    occupied = (jnp.arange(capacity, dtype=jnp.int32)[None, :] < arriving[:, None]).reshape(
        slot_count
    )
    grouped = fields.reshape(cells_across // 4, 4, cells_along // 4, 4, features)
    columns = (
        (jnp.sum(grouped, axis=(1, 3)) * 0.0625).reshape(own_cols, features).astype(jnp.bfloat16)
    )
    placer = (slot_of[None, :] == jnp.arange(slot_count, dtype=jnp.int32)[:, None]).astype(
        jnp.bfloat16
    )
    picks = placer
    outgoing = jnp.dot(
        picks,
        lax.all_gather(columns, "chan", axis=0, tiled=True),
        preferred_element_type=jnp.float32,
    )
    incoming = lax.all_to_all(
        outgoing.astype(jnp.bfloat16), "tile", split_axis=0, concat_axis=0, tiled=True
    )
    preact = lax.dot_general(
        w_hidden, incoming, (((0,), (1,)), ((), ())), preferred_element_type=jnp.float32
    )
    preact = preact + b_hidden[:, None]
    squash = jax.nn.sigmoid(preact)
    active = (preact * squash).astype(jnp.bfloat16)
    weights = w_radiance
    radiance = lax.dot_general(
        lax.all_gather(active, "chan", axis=0, tiled=True),
        weights,
        (((0,), (0,)), ((), ())),
        preferred_element_type=jnp.float32,
    )
    radiance = radiance + b_radiance[None, :]
    in_use = usable.astype(jnp.float32) * occupied.astype(jnp.float32)
    departure = ((radiance - observed.astype(jnp.float32)) * in_use[:, None]).astype(jnp.bfloat16)
    all_depart = lax.all_gather(departure, "chan", axis=1, tiled=True)
    picks = all_depart
    cotangent = jnp.dot(
        picks,
        lax.all_gather(inv_cov, "tile", axis=0, tiled=True),
        preferred_element_type=jnp.float32,
    )
    cotangent = cotangent.astype(jnp.bfloat16)
    weights = w_radiance
    full_sum = lax.psum(
        lax.dot_general(
            weights, cotangent, (((1,), (1,)), ((), ())), preferred_element_type=jnp.float32
        ),
        "chan",
    )
    grad_hidden = lax.dynamic_slice_in_dim(full_sum, chan_index * hidden_dev, hidden_dev, 0)
    slope_term = squash * (1.0 + preact * (1.0 - squash))
    grad_pre = (grad_hidden * slope_term).astype(jnp.bfloat16)
    part_grad = lax.dot_general(
        grad_pre, w_hidden, (((0,), (1,)), ((), ())), preferred_element_type=jnp.float32
    )
    summed_grad = lax.psum(part_grad, "chan")
    returned = lax.all_to_all(summed_grad, "tile", split_axis=0, concat_axis=0, tiled=True)
    own_slots = lax.dynamic_slice_in_dim(slot_of, chan_index * own_cols, own_cols, 0)
    column_grad = jnp.take(returned, own_slots, axis=0)
    spread = jnp.repeat(
        column_grad.reshape(cells_across // 4, cells_along // 4, features), 4, axis=0
    )
    adjoint = jnp.repeat(spread, 4, axis=1) * 0.0625
    kappa_root = jnp.sqrt(diffusivity)
    root_rim = add_rims(kappa_root)
    coef_north = (kappa_root * root_rim[2:, 1:-1])[:, :, None]
    coef_south = (kappa_root * root_rim[:-2, 1:-1])[:, :, None]
    coef_east = (kappa_root * root_rim[1:-1, 2:])[:, :, None]
    coef_west = (kappa_root * root_rim[1:-1, :-2])[:, :, None]
    for sweep_index in range(2):
        padded = add_rims(adjoint)
        adjoint = (
            adjoint
            + coef_north * (padded[2:, 1:-1] - adjoint)
            + coef_south * (padded[:-2, 1:-1] - adjoint)
            + coef_east * (padded[1:-1, 2:] - adjoint)
            + coef_west * (padded[1:-1, :-2] - adjoint)
        )
    return adjoint


def solution(mesh):
    placed = (
        P("chan", "tile", None),
        P("chan", "tile"),
        P(),
        P("tile", "chan"),
        P("tile"),
        P(None, "chan"),
        P("chan"),
        P(None, "chan"),
        P("chan"),
        P("tile", "chan"),
    )
    return jax.shard_map(
        body, mesh=mesh, in_specs=placed, out_specs=P("chan", "tile", None), check_vma=False
    )
```

profile of v0, /device:TPU:6, one launch (start us, length us, event | category | flops | bytes accessed | tf_op | source)
XLA Modules:
  0.0 599.1 jit_solution(5220718163068988109)
XLA Ops:
  6.6 0.9 copy.26
  7.5 1.0 reduce_sum.35
  8.6 3.3 convert_reduce_fusion
  12.0 26.5 %all_gather.12 = bf16[128,411]{1,0:T(8,128)(2,1)S(1)} all-gather(bf16[8,411]{1,0:T(8,128)(2,1)S(1)} %multiply_convert_fusion.3), channel_id=1, replica_groups=mesh['tile'=32,'chan'=16] {'chan'}, dimensions={0}, use_global_device_ids=true | all-gather | bytes 111792 | tf_op jit(solution)/shard_map/all_gather | solution.py:70
  38.5 0.2 dynamic-slice_reduce_fusion
  38.6 0.3 convolution_convert_fusion
  38.9 0.1 copy.29
  39.1 35.1 %all_to_all.24 = bf16[32,8,411]{2,1,0:T(8,128)(2,1)S(1)} all-to-all(bf16[32,8,411]{2,1,0:T(8,128)(2,1)S(1)} %bitcast.26), channel_id=1, replica_groups=mesh['tile'=32,'chan'=16] {'tile'}, dimensions={0} | all-to-all | bytes 420864 | tf_op jit(solution)/shard_map/all_to_all | solution.py:73
  74.2 0.9 multiply_convert_fusion.1
  75.2 0.2 dynamic-slice_reduce_fusion.1
  75.3 0.1 iota_compare_fusion.4
  75.4 0.1 lt.53
  75.5 47.4 %all-gather.4.cloned.1.call-done = bf16[2048,256]{0,1:T(8,128)(2,1)} async-done(((bf16[128,256]{0,1:T(8,128)(2,1)}), bf16[2048,256]{0,1:T(8,128)(2,1)}) %all-gather.4.cloned.1.call-update) | async-done | bytes 1048592 | tf_op jit(solution)/shard_map/all_gather | solution.py:84
  122.9 2.6 fusion.6
  125.6 0.7 all-gather.8.cloned.1.call-update
  126.3 66.2 %all-gather.6.cloned.1.call-done = bf16[256,6144]{1,0:T(8,128)(2,1)} async-done(((bf16[256,384]{1,0:T(8,128)(2,1)}), bf16[256,6144]{1,0:T(8,128)(2,1)}) %all-gather.6.cloned.1.call-update) | async-done | bytes 3145744 | tf_op jit(solution)/shard_map/all_gather | solution.py:92
  192.5 75.9 %all-gather.8.cloned.1.call-done = bf16[6144,384]{1,0:T(8,128)(2,1)} async-done(((bf16[192,384]{1,0:T(8,128)(2,1)}), bf16[6144,384]{1,0:T(8,128)(2,1)}) %all-gather.8.cloned.1.call-update) | async-done | bytes 4718608 | tf_op jit(solution)/shard_map/all_gather | solution.py:96
  268.4 7.1 %convolution_bitcast_fusion = f32[2048,256]{0,1:T(8,128)} fusion(bf16[2048,384]{1,0:T(8,128)(2,1)S(1)} %copy-done, bf16[256,6144]{1,0:T(8,128)(2,1)} %all-gather.6.cloned.1.call-done, bf16[6144,384]{1,0:T(8,128)(2,1)} %all-gather.8.cloned.1.call-done), kind=kOutput, calls=%fused_computation.5 | convolution fusion | flops 1610711040 | bytes 11534336 | tf_op jit(solution)/shard_map/dot_general | solution.py:102
  275.6 118.8 %all-reduce.3.cloned.1.call-done = f32[2048,256]{0,1:T(8,128)} async-done(((f32[2048,256]{0,1:T(8,128)}), f32[2048,256]{0,1:T(8,128)}) %all-reduce.3.cloned.1.call-update) | async-done | bytes 2097168 | tf_op jit(solution)/shard_map/psum | solution.py:101
  394.4 2.0 convolution_bitcast_fusion.1
  396.3 117.1 %all-reduce.5.cloned.1.call-done = f32[32,8,411]{2,1,0:T(8,128)} async-done(((f32[32,8,411]{2,1,0:T(8,128)}), f32[32,8,411]{2,1,0:T(8,128)}) %all-reduce.5.cloned.1.call-update) | async-done | bytes 420880 | tf_op jit(solution)/shard_map/psum | solution.py:113
  513.4 12.6 %all-to-all-start.1 = ((f32[32,8,411]{2,1,0:T(8,128)}), f32[32,8,411]{2,1,0:T(8,128)S(1)}, u32[]{:S(2)}, u32[]{:S(2)}) async-start(f32[32,8,411]{2,1,0:T(8,128)} %all-reduce.5.cloned.1.call-done), calls=%async_computation.1 | async-start | bytes 1048576 | tf_op jit(solution)/shard_map/all_to_all | solution.py:114
  526.1 3.4 collective-permute-start.2
  529.4 2.5 collective-permute-start
  531.9 0.2 dynamic-slice_reduce_fusion.2
  532.2 4.8 collective-permute-done
  537.0 0.1 fusion.40
  537.1 1.7 collective-permute-start.4
  538.8 21.3 %all-to-all-done.1 = f32[32,8,411]{2,1,0:T(8,128)S(1)} async-done(((f32[32,8,411]{2,1,0:T(8,128)}), f32[32,8,411]{2,1,0:T(8,128)S(1)}, u32[]{:S(2)}, u32[]{:S(2)}) %all-to-all-start.1) | async-done | bytes 420896 | tf_op jit(solution)/shard_map/all_to_all | solution.py:114
  560.0 0.6 gather_fusion
  560.6 0.1 select_multiply_fusion
  560.7 3.4 collective-permute-start.3
  564.1 2.5 collective-permute-start.1
  566.6 0.1 pad_maximum_fusion.25
  566.7 0.2 collective-permute-done.3
  566.9 5.5 collective-permute-done.1
  572.5 0.5 collective-permute-start.7
  573.0 0.8 collective-permute-done.5
  573.9 2.9 collective-permute-done.7
  576.8 0.2 fusion.23
  577.0 1.9 collective-permute-start.9
  579.0 3.9 collective-permute-start.8
  582.9 0.3 collective-permute-done.9
  583.2 4.0 collective-permute-done.8
  587.3 0.5 collective-permute-start.11
  587.8 0.9 collective-permute-done.10
  588.7 2.9 collective-permute-done.11
  591.6 0.9 fusion.11
  (49 shorter events, 0.7 us)
Async XLA Ops:
  6.5 116.4 %copy-start = (bf16[2048,384]{1,0:T(8,128)(2,1)S(1)}, bf16[2048,384]{1,0:T(8,128)(2,1)}, u32[]{:S(2)}) copy-start(bf16[2048,384]{1,0:T(8,128)(2,1)} %param.17) | copy-start | bytes 4718596
  6.5 67.7 %copy-start.1 = (bf16[411,128]{1,0:T(8,128)(2,1)S(1)}, bf16[411,128]{1,0:T(8,128)(2,1)}, u32[]{:S(2)}) copy-start(bf16[411,128]{1,0:T(8,128)(2,1)} %param.15) | copy-start | bytes 315652
  6.5 67.7 %copy-start.6 = (f32[128]{0:T(128)S(1)}, f32[128]{0:T(128)}, u32[]{:S(2)}) copy-start(f32[128]{0:T(128)} %param.16) | copy-start | bytes 1540
  6.5 69.0 %copy-start.3 = (s32[256]{0:T(256)S(1)}, s32[256]{0:T(256)}, u32[]{:S(2)}) copy-start(s32[256]{0:T(256)} %param.14) | copy-start | bytes 3076
  6.5 116.4 %copy-start.5 = (f32[384]{0:T(512)S(1)}, f32[384]{0:T(512)}, u32[]{:S(2)}) copy-start(f32[384]{0:T(512)} %param.18) | copy-start | bytes 4612
  6.5 116.4 %copy-start.4 = (bf16[256,384]{1,0:T(8,128)(2,1)S(1)}, bf16[256,384]{1,0:T(8,128)(2,1)}, u32[]{:S(2)}) copy-start(bf16[256,384]{1,0:T(8,128)(2,1)} %param.13) | copy-start | bytes 589828
  6.6 116.4 %all-gather.4.cloned.1.call-start = ((), (), s32[]{:S(2)}) async-start(), calls=%async_computation.2 | async-start | bytes 1114112 | tf_op jit(solution)/shard_map/all_gather | solution.py:84
  75.1 117.4 %all-gather.6.cloned.1.call-start = ((), (), s32[]{:S(2)}) async-start(), calls=%async_computation.3 | async-start | bytes 3342336 | tf_op jit(solution)/shard_map/all_gather | solution.py:92
  125.6 142.8 %all-gather.8.cloned.1.call-start = ((), (), s32[]{:S(2)}) async-start(), calls=%async_computation.4 | async-start | bytes 4866048 | tf_op jit(solution)/shard_map/all_gather | solution.py:96
  126.3 268.1 %all-reduce.3.cloned.1.call-start = ((), (), s32[]{:S(2)}) async-start(), calls=%async_computation.5 | async-start | bytes 4194304 | tf_op jit(solution)/shard_map/psum | solution.py:101
  275.5 250.5 %copy-start.2 = (f32[4,32]{1,0:T(4,128)S(1)}, f32[4,32]{1,0:T(4,128)}, u32[]{:S(2)}) copy-start(f32[4,32]{1,0:T(4,128)} %param.11) | copy-start | bytes 1540
  275.5 237.9 %all-reduce.5.cloned.1.call-start = ((), (), s32[]{:S(2)}) async-start(), calls=%async_computation.6 | async-start | bytes 1048576 | tf_op jit(solution)/shard_map/psum | solution.py:113
  513.4 46.6 %all-to-all-start.1 = ((f32[32,8,411]{2,1,0:T(8,128)}), f32[32,8,411]{2,1,0:T(8,128)S(1)}, u32[]{:S(2)}, u32[]{:S(2)}) async-start(f32[32,8,411]{2,1,0:T(8,128)} %all-reduce.5.cloned.1.call-done), calls=%async_computation.1 | async-start | bytes 1048576 | tf_op jit(solution)/shard_map/all_to_all | solution.py:114
  526.1 6.1 %collective-permute-start.2 = (f32[1,32]{1,0:T(1,128)S(1)}, f32[1,32]{1,0:T(1,128)S(1)}, u32[]{:S(2)}, u32[]{:S(2)}) collective-permute-start(f32[1,32]{1,0:T(1,128)S(1)} %get-tuple-element.23), channel_id=1, source_target_pairs={{0,1},{1,2},{2,3},{3,4},{4,5},{5,6},{6,7},{7,8},{8,9},{9,10},{10,1... | collective-permute-start | bytes 392 | tf_op jit(solution)/shard_map/ppermute | solution.py:14
  529.4 7.6 %collective-permute-start = (f32[1,32]{1,0:T(1,128)S(1)}, f32[1,32]{1,0:T(1,128)S(1)}, u32[]{:S(2)}, u32[]{:S(2)}) collective-permute-start(f32[1,32]{1,0:T(1,128)S(1)} %get-tuple-element.24), channel_id=1, source_target_pairs={{1,0},{2,1},{3,2},{4,3},{5,4},{6,5},{7,6},{8,7},{9,8},{10,9},{11,1... | collective-permute-start | bytes 392 | tf_op jit(solution)/shard_map/ppermute | solution.py:15
  537.1 29.5 %collective-permute-start.4 = (f32[6,1]{1,0:T(8,128)S(1)}, f32[6,1]{1,0:T(8,128)S(1)}, u32[]{:S(2)}, u32[]{:S(2)}) collective-permute-start(f32[6,1]{1,0:T(8,128)S(1)} %get-tuple-element.13), channel_id=1, source_target_pairs={{16,0},{32,16},{48,32},{64,48},{80,64},{96,80},{112,96},{128,112},... | collective-permute-start | bytes 80 | tf_op jit(solution)/shard_map/ppermute | solution.py:15
  538.8 27.8 %collective-permute-start.6 = (f32[6,1]{1,0:T(8,128)S(1)}, f32[6,1]{1,0:T(8,128)S(1)}, u32[]{:S(2)}, u32[]{:S(2)}) collective-permute-start(f32[6,1]{1,0:T(8,128)S(1)} %get-tuple-element.14), channel_id=1, source_target_pairs={{0,16},{16,32},{32,48},{48,64},{64,80},{80,96},{96,112},{112,128},... | collective-permute-start | bytes 80 | tf_op jit(solution)/shard_map/ppermute | solution.py:14
  560.7 6.2 %collective-permute-start.3 = (f32[1,32,411]{2,1,0:T(8,128)S(1)}, f32[1,32,411]{2,1,0:T(8,128)S(1)}, u32[]{:S(2)}, u32[]{:S(2)}) collective-permute-start(f32[1,32,411]{2,1,0:T(8,128)S(1)} %mul.151), channel_id=1, source_target_pairs={{0,1},{1,2},{2,3},{3,4},{4,5},{5,6},{6,7},{7,8},{8,9},{9,10},{10,1... | collective-permute-start | bytes 157832 | tf_op jit(solution)/shard_map/ppermute | solution.py:14
  564.1 8.3 %collective-permute-start.1 = (f32[1,32,411]{2,1,0:T(8,128)S(1)}, f32[1,32,411]{2,1,0:T(8,128)S(1)}, u32[]{:S(2)}, u32[]{:S(2)}) collective-permute-start(f32[1,32,411]{2,1,0:T(8,128)S(1)} %mul.151), channel_id=1, source_target_pairs={{1,0},{2,1},{3,2},{4,3},{5,4},{6,5},{7,6},{8,7},{9,8},{10,9},{11,1... | collective-permute-start | bytes 157832 | tf_op jit(solution)/shard_map/ppermute | solution.py:15
  572.4 1.4 collective-permute-start.5
  572.5 4.3 collective-permute-start.7
  577.0 6.2 %collective-permute-start.9 = (f32[1,32,411]{2,1,0:T(8,128)S(1)}, f32[1,32,411]{2,1,0:T(8,128)S(1)}, u32[]{:S(2)}, u32[]{:S(2)}) collective-permute-start(f32[1,32,411]{2,1,0:T(8,128)S(1)} %get-tuple-element.11), channel_id=1, source_target_pairs={{0,1},{1,2},{2,3},{3,4},{4,5},{5,6},{6,7},{7,8},{8,9},{9,10},{10,1... | collective-permute-start | bytes 157832 | tf_op jit(solution)/shard_map/ppermute | solution.py:14
  579.0 8.3 %collective-permute-start.8 = (f32[1,32,411]{2,1,0:T(8,128)S(1)}, f32[1,32,411]{2,1,0:T(8,128)S(1)}, u32[]{:S(2)}, u32[]{:S(2)}) collective-permute-start(f32[1,32,411]{2,1,0:T(8,128)S(1)} %get-tuple-element.12), channel_id=1, source_target_pairs={{1,0},{2,1},{3,2},{4,3},{5,4},{6,5},{7,6},{8,7},{9,8},{10,9},{11,1... | collective-permute-start | bytes 157832 | tf_op jit(solution)/shard_map/ppermute | solution.py:15
  587.3 1.4 collective-permute-start.10
  587.3 4.3 collective-permute-start.11
Sparse Core Ops, SparseCore 0:
  75.2 47.6 all-gather.3
  125.9 66.5 all-gather.5
  194.7 73.6 all-gather.7
  275.7 118.6 all-reduce.2
  397.4 115.9 all-reduce.4
where the time goes:
time: 600 us; the launch traced here: 599 us
  waiting for transfers between devices  470 us (78%)
  blocking collectives  61.6 us (10%)
  starting transfers between devices  33 us (6%)
  between operations  13.5 us (2%)
  matrix products  12.8 us (2%)
    psum x1, waiting for transfers between devices, body(): lax.psum(lax.dot_general(weights, cotangent, (((1,), (1,)), ((), ())), pr...  119 us
    psum x1, waiting for transfers between devices, body(): summed_grad = lax.psum(part_grad, 'chan')  117 us
    all_gather x1, waiting for transfers between devices, body(): lax.all_gather(inv_cov, 'tile', axis=0, tiled=True)  75.9 us
    all_gather x1, waiting for transfers between devices, body(): all_depart = lax.all_gather(departure, 'chan', axis=1, tiled=True)  66.2 us
    all_gather x1, waiting for transfers between devices, body(): lax.all_gather(active, 'chan', axis=0, tiled=True)  47.4 us
    all_to_all x1, blocking collectives, body(): lax.all_to_all(outgoing.astype(jnp.bfloat16), 'tile', split_axis=0, conca...  35.1 us
    all_gather x1, blocking collectives, body(): lax.all_gather(columns, 'chan', axis=0, tiled=True)  26.5 us
    all_to_all x1, waiting for transfers between devices, body(): lax.all_to_all(summed_grad, 'tile', split_axis=0, concat_axis=0, tiled=True)  21.3 us
  transfers between devices with their start and end apart: 18, of which 15 were waited for; matrix products, arithmetic and copies ran while one was open for 0% of the time, Pallas kernels for 0%

commit v1 on v0

--- a/solution.py
+++ b/solution.py
@@ -81,7 +81,9 @@
     active = (preact * squash).astype(jnp.bfloat16)
     weights = w_radiance
     radiance = lax.dot_general(
-        lax.all_gather(active, "chan", axis=0, tiled=True),
+        jnp.concatenate(
+            lax.all_to_all(jnp.stack([active] * lax.axis_size("chan")), "chan", 0, 0), axis=0
+        ),
         weights,
         (((0,), (0,)), ((), ())),
         preferred_element_type=jnp.float32,

time: 600 us -> 563 us (0.938)
  waiting for transfers between devices: 470 us -> 428 us
    all_gather x1 -> x0, waiting for transfers between devices: 47.4 us -> none  [body(): lax.all_gather(active, 'chan', axis=0, tiled=True)]
    all_to_all x0 -> x1, waiting for transfers between devices: none -> 14.1 us  [body(): lax.all_to_all(jnp.stack([active] * lax.axis_size('chan')), 'chan', 0, 0)]
    all_gather x1, waiting for transfers between devices: 66.2 us -> 57.9 us  [body(): all_depart = lax.all_gather(departure, 'chan', axis=1, tiled=True)]
where the time goes in v1:
time: 563 us
  waiting for transfers between devices  428 us (76%)
  blocking collectives  61.6 us (11%)
  starting transfers between devices  38.7 us (7%)
  between operations  13.5 us (2%)
  matrix products  11 us (2%)
  other arithmetic  5.88 us (1%)
    psum x1, waiting for transfers between devices, body(): lax.psum(lax.dot_general(weights, cotangent, (((1,), (1,)), ((), ())), pr...  119 us
    psum x1, waiting for transfers between devices, body(): summed_grad = lax.psum(part_grad, 'chan')  117 us
    all_gather x1, waiting for transfers between devices, body(): lax.all_gather(inv_cov, 'tile', axis=0, tiled=True)  75.9 us
    all_gather x1, waiting for transfers between devices, body(): all_depart = lax.all_gather(departure, 'chan', axis=1, tiled=True)  57.9 us
    all_to_all x1, blocking collectives, body(): lax.all_to_all(outgoing.astype(jnp.bfloat16), 'tile', split_axis=0, conca...  35.1 us
    all_gather x1, blocking collectives, body(): lax.all_gather(columns, 'chan', axis=0, tiled=True)  26.5 us
    all_to_all x1, waiting for transfers between devices, body(): lax.all_to_all(summed_grad, 'tile', split_axis=0, concat_axis=0, tiled=True)  21.3 us
    ppermute x6, waiting for transfers between devices, padded_2(): after = lax.ppermute(first, axis, down)  16.1 us
  transfers between devices with their start and end apart: 18, of which 15 were waited for; matrix products, arithmetic and copies ran while one was open for 0% of the time, Pallas kernels for 0%

profile of v1, /device:TPU:6, one launch (start us, length us, event | category | flops | bytes accessed | tf_op | source)
XLA Modules:
  0.0 562.6 jit_solution(10974468841178897335)
XLA Ops:
  6.5 0.9 copy.31
  7.5 1.0 reduce_sum.35
  8.6 3.3 convert_reduce_fusion
  11.9 26.5 %all_gather.9 = bf16[128,411]{1,0:T(8,128)(2,1)S(1)} all-gather(bf16[8,411]{1,0:T(8,128)(2,1)S(1)} %multiply_convert_fusion.3), channel_id=1, replica_groups=mesh['tile'=32,'chan'=16] {'chan'}, dimensions={0}, use_global_device_ids=true | all-gather | bytes 111792 | tf_op jit(solution)/shard_map/all_gather | solution.py:70
  38.4 0.2 dynamic-slice_reduce_fusion
  38.6 0.3 convolution_convert_fusion
  38.9 0.1 copy.34
  39.0 35.1 %all_to_all.29 = bf16[32,8,411]{2,1,0:T(8,128)(2,1)S(1)} all-to-all(bf16[32,8,411]{2,1,0:T(8,128)(2,1)S(1)} %bitcast.28), channel_id=1, replica_groups=mesh['tile'=32,'chan'=16] {'tile'}, dimensions={0} | all-to-all | bytes 420864 | tf_op jit(solution)/shard_map/all_to_all | solution.py:73
  74.2 0.2 multiply_convert_fusion.1
  74.4 0.1 copy.35
  74.5 1.1 stack.2
  75.6 5.7 %all-to-all-start.1 = ((bf16[16,128,256]{2,1,0:T(8,128)(2,1)}), bf16[16,128,256]{2,1,0:T(8,128)(2,1)S(1)}, u32[]{:S(2)}, u32[]{:S(2)}) async-start(bf16[16,128,256]{2,1,0:T(8,128)(2,1)} %stack.2), calls=%async_computation.1 | async-start | bytes 2097152 | tf_op jit(solution)/shard_map/all_to_all | solution.py:85
  81.3 0.2 dynamic-slice_reduce_fusion.1
  81.6 0.1 lt.53
  81.7 14.1 %all-to-all-done.1 = bf16[16,128,256]{2,1,0:T(8,128)(2,1)S(1)} async-done(((bf16[16,128,256]{2,1,0:T(8,128)(2,1)}), bf16[16,128,256]{2,1,0:T(8,128)(2,1)S(1)}, u32[]{:S(2)}, u32[]{:S(2)}) %all-to-all-start.1) | async-done | bytes 1048608 | tf_op jit(solution)/shard_map/all_to_all | solution.py:85
  95.8 1.4 fusion.6
  97.3 0.7 all-gather.5.cloned.1.call-update
  98.1 57.9 %all-gather.3.cloned.1.call-done = bf16[256,6144]{1,0:T(8,128)(2,1)} async-done(((bf16[256,384]{1,0:T(8,128)(2,1)}), bf16[256,6144]{1,0:T(8,128)(2,1)}) %all-gather.3.cloned.1.call-update) | async-done | bytes 3145744 | tf_op jit(solution)/shard_map/all_gather | solution.py:94
  156.0 75.9 %all-gather.5.cloned.1.call-done = bf16[6144,384]{1,0:T(8,128)(2,1)} async-done(((bf16[192,384]{1,0:T(8,128)(2,1)}), bf16[6144,384]{1,0:T(8,128)(2,1)}) %all-gather.5.cloned.1.call-update) | async-done | bytes 4718608 | tf_op jit(solution)/shard_map/all_gather | solution.py:98
  231.9 7.1 %convolution_bitcast_fusion = f32[2048,256]{0,1:T(8,128)} fusion(bf16[2048,384]{1,0:T(8,128)(2,1)S(1)} %copy-done, bf16[256,6144]{1,0:T(8,128)(2,1)} %all-gather.3.cloned.1.call-done, bf16[6144,384]{1,0:T(8,128)(2,1)} %all-gather.5.cloned.1.call-done), kind=kOutput, calls=%fused_computation.5 | convolution fusion | flops 1610711040 | bytes 11534336 | tf_op jit(solution)/shard_map/dot_general | solution.py:104
  239.1 118.8 %all-reduce.3.cloned.1.call-done = f32[2048,256]{0,1:T(8,128)} async-done(((f32[2048,256]{0,1:T(8,128)}), f32[2048,256]{0,1:T(8,128)}) %all-reduce.3.cloned.1.call-update) | async-done | bytes 2097168 | tf_op jit(solution)/shard_map/psum | solution.py:103
  357.8 1.9 convolution_bitcast_fusion.1
  359.8 117.1 %all-reduce.5.cloned.1.call-done = f32[32,8,411]{2,1,0:T(8,128)} async-done(((f32[32,8,411]{2,1,0:T(8,128)}), f32[32,8,411]{2,1,0:T(8,128)}) %all-reduce.5.cloned.1.call-update) | async-done | bytes 420880 | tf_op jit(solution)/shard_map/psum | solution.py:115
  476.9 12.6 %all-to-all-start.2 = ((f32[32,8,411]{2,1,0:T(8,128)}), f32[32,8,411]{2,1,0:T(8,128)S(1)}, u32[]{:S(2)}, u32[]{:S(2)}) async-start(f32[32,8,411]{2,1,0:T(8,128)} %all-reduce.5.cloned.1.call-done), calls=%async_computation.2 | async-start | bytes 1048576 | tf_op jit(solution)/shard_map/all_to_all | solution.py:116
  489.5 3.4 collective-permute-start.2
  492.9 2.5 collective-permute-start
  495.4 0.2 dynamic-slice_reduce_fusion.2
  495.6 4.8 collective-permute-done
  500.6 1.7 collective-permute-start.4
  502.3 21.3 %all-to-all-done.2 = f32[32,8,411]{2,1,0:T(8,128)S(1)} async-done(((f32[32,8,411]{2,1,0:T(8,128)}), f32[32,8,411]{2,1,0:T(8,128)S(1)}, u32[]{:S(2)}, u32[]{:S(2)}) %all-to-all-start.2) | async-done | bytes 420896 | tf_op jit(solution)/shard_map/all_to_all | solution.py:116
  523.5 0.6 gather_fusion
  524.2 3.4 collective-permute-start.3
  527.6 2.5 collective-permute-start.1
  530.1 0.1 pad_maximum_fusion.25
  530.2 0.2 collective-permute-done.3
  530.4 5.5 collective-permute-done.1
  535.9 0.5 collective-permute-start.7
  536.5 0.8 collective-permute-done.5
  537.3 2.9 collective-permute-done.7
  540.3 0.2 fusion.23
  540.5 1.9 collective-permute-start.9
  542.4 3.9 collective-permute-start.8
  546.4 0.3 collective-permute-done.9
  546.7 4.0 collective-permute-done.8
  550.8 0.5 collective-permute-start.11
  551.3 0.9 collective-permute-done.10
  552.2 2.9 collective-permute-done.11
  555.1 0.9 fusion.11
  (50 shorter events, 0.8 us)
Async XLA Ops:
  6.5 89.3 %copy-start = (bf16[2048,384]{1,0:T(8,128)(2,1)S(1)}, bf16[2048,384]{1,0:T(8,128)(2,1)}, u32[]{:S(2)}) copy-start(bf16[2048,384]{1,0:T(8,128)(2,1)} %param.17) | copy-start | bytes 4718596
  6.5 67.6 %copy-start.2 = (bf16[411,128]{1,0:T(8,128)(2,1)S(1)}, bf16[411,128]{1,0:T(8,128)(2,1)}, u32[]{:S(2)}) copy-start(bf16[411,128]{1,0:T(8,128)(2,1)} %param.15) | copy-start | bytes 315652
  6.5 67.6 %copy-start.6 = (f32[128]{0:T(128)S(1)}, f32[128]{0:T(128)}, u32[]{:S(2)}) copy-start(f32[128]{0:T(128)} %param.16) | copy-start | bytes 1540
  74.1 7.6 %copy-start.5 = (s32[256]{0:T(256)S(1)}, s32[256]{0:T(256)}, u32[]{:S(2)}) copy-start(s32[256]{0:T(256)} %param.14) | copy-start | bytes 3076
  74.1 21.7 %copy-start.1 = (bf16[256,384]{1,0:T(8,128)(2,1)S(1)}, bf16[256,384]{1,0:T(8,128)(2,1)}, u32[]{:S(2)}) copy-start(bf16[256,384]{1,0:T(8,128)(2,1)} %param.13) | copy-start | bytes 589828
  74.2 21.7 %copy-start.3 = (f32[384]{0:T(512)S(1)}, f32[384]{0:T(512)}, u32[]{:S(2)}) copy-start(f32[384]{0:T(512)} %param.18) | copy-start | bytes 4612
  75.6 20.2 %all-to-all-start.1 = ((bf16[16,128,256]{2,1,0:T(8,128)(2,1)}), bf16[16,128,256]{2,1,0:T(8,128)(2,1)S(1)}, u32[]{:S(2)}, u32[]{:S(2)}) async-start(bf16[16,128,256]{2,1,0:T(8,128)(2,1)} %stack.2), calls=%async_computation.1 | async-start | bytes 2097152 | tf_op jit(solution)/shard_map/all_to_all | solution.py:85
  81.3 74.7 %all-gather.3.cloned.1.call-start = ((), (), s32[]{:S(2)}) async-start(), calls=%async_computation.3 | async-start | bytes 3342336 | tf_op jit(solution)/shard_map/all_gather | solution.py:94
  97.3 134.6 %all-gather.5.cloned.1.call-start = ((), (), s32[]{:S(2)}) async-start(), calls=%async_computation.4 | async-start | bytes 4866048 | tf_op jit(solution)/shard_map/all_gather | solution.py:98
  98.1 259.8 %all-reduce.3.cloned.1.call-start = ((), (), s32[]{:S(2)}) async-start(), calls=%async_computation.5 | async-start | bytes 4194304 | tf_op jit(solution)/shard_map/psum | solution.py:103
  239.0 250.5 %copy-start.4 = (f32[4,32]{1,0:T(4,128)S(1)}, f32[4,32]{1,0:T(4,128)}, u32[]{:S(2)}) copy-start(f32[4,32]{1,0:T(4,128)} %param.11) | copy-start | bytes 1540
  239.0 237.9 %all-reduce.5.cloned.1.call-start = ((), (), s32[]{:S(2)}) async-start(), calls=%async_computation.6 | async-start | bytes 1048576 | tf_op jit(solution)/shard_map/psum | solution.py:115
  476.9 46.6 %all-to-all-start.2 = ((f32[32,8,411]{2,1,0:T(8,128)}), f32[32,8,411]{2,1,0:T(8,128)S(1)}, u32[]{:S(2)}, u32[]{:S(2)}) async-start(f32[32,8,411]{2,1,0:T(8,128)} %all-reduce.5.cloned.1.call-done), calls=%async_computation.2 | async-start | bytes 1048576 | tf_op jit(solution)/shard_map/all_to_all | solution.py:116
  489.5 6.1 %collective-permute-start.2 = (f32[1,32]{1,0:T(1,128)S(1)}, f32[1,32]{1,0:T(1,128)S(1)}, u32[]{:S(2)}, u32[]{:S(2)}) collective-permute-start(f32[1,32]{1,0:T(1,128)S(1)} %get-tuple-element.23), channel_id=1, source_target_pairs={{0,1},{1,2},{2,3},{3,4},{4,5},{5,6},{6,7},{7,8},{8,9},{9,10},{10,1... | collective-permute-start | bytes 392 | tf_op jit(solution)/shard_map/ppermute | solution.py:14
  492.9 7.6 %collective-permute-start = (f32[1,32]{1,0:T(1,128)S(1)}, f32[1,32]{1,0:T(1,128)S(1)}, u32[]{:S(2)}, u32[]{:S(2)}) collective-permute-start(f32[1,32]{1,0:T(1,128)S(1)} %get-tuple-element.24), channel_id=1, source_target_pairs={{1,0},{2,1},{3,2},{4,3},{5,4},{6,5},{7,6},{8,7},{9,8},{10,9},{11,1... | collective-permute-start | bytes 392 | tf_op jit(solution)/shard_map/ppermute | solution.py:15
  500.6 29.5 %collective-permute-start.4 = (f32[6,1]{1,0:T(8,128)S(1)}, f32[6,1]{1,0:T(8,128)S(1)}, u32[]{:S(2)}, u32[]{:S(2)}) collective-permute-start(f32[6,1]{1,0:T(8,128)S(1)} %get-tuple-element.13), channel_id=1, source_target_pairs={{16,0},{32,16},{48,32},{64,48},{80,64},{96,80},{112,96},{128,112},... | collective-permute-start | bytes 80 | tf_op jit(solution)/shard_map/ppermute | solution.py:15
  502.2 27.8 %collective-permute-start.6 = (f32[6,1]{1,0:T(8,128)S(1)}, f32[6,1]{1,0:T(8,128)S(1)}, u32[]{:S(2)}, u32[]{:S(2)}) collective-permute-start(f32[6,1]{1,0:T(8,128)S(1)} %get-tuple-element.14), channel_id=1, source_target_pairs={{0,16},{16,32},{32,48},{48,64},{64,80},{80,96},{96,112},{112,128},... | collective-permute-start | bytes 80 | tf_op jit(solution)/shard_map/ppermute | solution.py:14
  524.2 6.2 %collective-permute-start.3 = (f32[1,32,411]{2,1,0:T(8,128)S(1)}, f32[1,32,411]{2,1,0:T(8,128)S(1)}, u32[]{:S(2)}, u32[]{:S(2)}) collective-permute-start(f32[1,32,411]{2,1,0:T(8,128)S(1)} %mul.151), channel_id=1, source_target_pairs={{0,1},{1,2},{2,3},{3,4},{4,5},{5,6},{6,7},{7,8},{8,9},{9,10},{10,1... | collective-permute-start | bytes 157832 | tf_op jit(solution)/shard_map/ppermute | solution.py:14
  527.6 8.3 %collective-permute-start.1 = (f32[1,32,411]{2,1,0:T(8,128)S(1)}, f32[1,32,411]{2,1,0:T(8,128)S(1)}, u32[]{:S(2)}, u32[]{:S(2)}) collective-permute-start(f32[1,32,411]{2,1,0:T(8,128)S(1)} %mul.151), channel_id=1, source_target_pairs={{1,0},{2,1},{3,2},{4,3},{5,4},{6,5},{7,6},{8,7},{9,8},{10,9},{11,1... | collective-permute-start | bytes 157832 | tf_op jit(solution)/shard_map/ppermute | solution.py:15
  535.9 1.4 collective-permute-start.5
  535.9 4.3 collective-permute-start.7
  540.5 6.2 %collective-permute-start.9 = (f32[1,32,411]{2,1,0:T(8,128)S(1)}, f32[1,32,411]{2,1,0:T(8,128)S(1)}, u32[]{:S(2)}, u32[]{:S(2)}) collective-permute-start(f32[1,32,411]{2,1,0:T(8,128)S(1)} %get-tuple-element.11), channel_id=1, source_target_pairs={{0,1},{1,2},{2,3},{3,4},{4,5},{5,6},{6,7},{7,8},{8,9},{9,10},{10,1... | collective-permute-start | bytes 157832 | tf_op jit(solution)/shard_map/ppermute | solution.py:14
  542.4 8.3 %collective-permute-start.8 = (f32[1,32,411]{2,1,0:T(8,128)S(1)}, f32[1,32,411]{2,1,0:T(8,128)S(1)}, u32[]{:S(2)}, u32[]{:S(2)}) collective-permute-start(f32[1,32,411]{2,1,0:T(8,128)S(1)} %get-tuple-element.12), channel_id=1, source_target_pairs={{1,0},{2,1},{3,2},{4,3},{5,4},{6,5},{7,6},{8,7},{9,8},{10,9},{11,1... | collective-permute-start | bytes 157832 | tf_op jit(solution)/shard_map/ppermute | solution.py:15
  550.7 1.4 collective-permute-start.10
  550.8 4.3 collective-permute-start.11
Sparse Core Ops, SparseCore 0:
  97.4 58.5 all-gather.2
  158.1 73.6 all-gather.4
  239.1 118.6 all-reduce.2
  360.9 115.9 all-reduce.4
